TPU v7x, 128 devices: a whole 4x4x4 slice. The times are simulated.
128 devices in a mesh: heads: 8 (over z, core), width: 4 (over y), sae: 4 (over x).
Axes of the slice: x: 4, y: 4, z: 4, core: 2. Of those that a mesh axis runs over, the one named last changes fastest.
Arguments:
- x_in: bfloat16 [512, 4608], P(None, 'width'), may hold values from -64 to 64
- doc_lengths: int32 [4], replicated, may hold values from 1 to 256, 512 in all
- attn_gain: float32 [4608], P('width'), may hold values from 0.25 to 1.75
- w_query: bfloat16 [4608, 4096], P('width', 'heads'), may hold values from -0.09375 to 0.09375
- w_key: bfloat16 [4608, 2048], P('width', 'heads'), may hold values from -0.09375 to 0.09375
- w_value: bfloat16 [4608, 2048], P('width', 'heads'), may hold values from -0.09375 to 0.09375
- w_out: bfloat16 [4096, 4608], P('heads', 'width'), may hold values from -0.09375 to 0.09375
- post_gain: float32 [4608], replicated, may hold values from 0.25 to 1.75
- enc_weight: bfloat16 [4608, 65536], P(None, ('heads', 'width', 'sae')), may hold values from -0.09375 to 0.09375
- enc_bias: float32 [65536], P(('heads', 'width', 'sae')), may hold values from -1.5 to 0.5
- dec_weight: bfloat16 [65536, 4608], P(('heads', 'width', 'sae')), may hold values from -1 to 1
- dec_bias: float32 [4608], replicated, may hold values from -5 to 5
Outputs:
- grad_enc: bfloat16 [4608, 65536], P(None, ('heads', 'width', 'sae'))
- grad_dec: bfloat16 [65536, 4608], P(('heads', 'width', 'sae'))
- total_loss: float32 [], replicated
Inputs may be any that keep to these rules, and one draw needn't show every extreme that they name: `doc_lengths`: lengths of the 4 documents packed in order; they sum to 512.
All inputs are finite; a program needn't handle non-finite values.
Results may differ from a plain program's by a relative error of at most 0.02.
Values may be sent and summed in bfloat16 or wider, within the bound.
A program may use at most 128 MiB of HBM per device.

v0:
```python
import jax
import jax.numpy as jnp
from jax import lax
from jax.sharding import PartitionSpec as P

D = 4608
HEADS = 32
HEAD_DIM = 128
norm_eps = 1e-06
soft_cap = 50.0
rope_base = 10000.0
l1_weight = 3.0


def rotary(values, position):
    half_dim = values.shape[-1] // 2
    frequency = rope_base ** (-2.0 * jnp.arange(half_dim, dtype=jnp.float32) / values.shape[-1])
    angles = position.astype(jnp.float32)[:, None] * frequency[None, :]
    cosine_table = jnp.cos(angles)[:, None, :]
    sine_table = jnp.sin(angles)[:, None, :]
    first_half = values[..., :half_dim]
    second_half = values[..., half_dim:]
    return jnp.concatenate(
        [
            first_half * cosine_table - second_half * sine_table,
            second_half * cosine_table + first_half * sine_table,
        ],
        axis=-1,
    )


def attend_rows(query_rows, key_rows, value_rows, allowed_rows, scale):
    scores = (
        jnp.einsum("tkgd,skd->kgts", query_rows, key_rows, preferred_element_type=jnp.float32)
        * scale
    )
    capped = soft_cap * jnp.tanh(scores / soft_cap)
    weights = jnp.where(allowed_rows[None, None], jnp.exp(capped), 0.0)
    totals = jnp.sum(weights, axis=-1, keepdims=True)
    probs_bf = (weights / totals).astype(jnp.bfloat16)
    return jnp.einsum(
        "kgts,skd->tkgd", probs_bf, value_rows, preferred_element_type=jnp.float32
    ).astype(jnp.bfloat16)


def per_device(
    x_in,
    doc_lengths,
    attn_gain,
    w_query,
    w_key,
    w_value,
    w_out,
    post_gain,
    enc_weight,
    enc_bias,
    dec_weight,
    dec_bias,
):
    tokens = x_in.shape[0]
    query_heads = w_query.shape[1] // HEAD_DIM
    value_heads = w_key.shape[1] // HEAD_DIM
    boundary = jnp.cumsum(doc_lengths)
    position = jnp.arange(tokens, dtype=jnp.int32)
    segment = jnp.sum((boundary[None, :] <= position[:, None]).astype(jnp.int32), axis=1)
    allowed = (segment[:, None] == segment[None, :]) & (position[None, :] <= position[:, None])
    x_float = x_in.astype(jnp.float32)
    scaled = (x_float * attn_gain).astype(jnp.bfloat16)
    query_part = jnp.dot(scaled, w_query, preferred_element_type=jnp.float32)
    key_part = jnp.dot(scaled, w_key, preferred_element_type=jnp.float32)
    value_part = jnp.dot(scaled, w_value, preferred_element_type=jnp.float32)
    square_part = jnp.sum(x_float * x_float, axis=1)
    query_raw, key_raw, value_raw, square_sums = lax.psum(
        (query_part, key_part, value_part, square_part), "width"
    )
    inverse_rms = lax.rsqrt(square_sums / D + norm_eps)
    query = rotary(
        (query_raw * inverse_rms[:, None]).reshape(tokens, query_heads, HEAD_DIM), position
    ).astype(jnp.bfloat16)
    key_rows = rotary(
        (key_raw * inverse_rms[:, None]).reshape(tokens, value_heads, HEAD_DIM), position
    ).astype(jnp.bfloat16)
    value_rows = (
        (value_raw * inverse_rms[:, None])
        .reshape(tokens, value_heads, HEAD_DIM)
        .astype(jnp.bfloat16)
    )
    query4 = query.reshape(tokens, value_heads, query_heads // value_heads, HEAD_DIM)
    pieces_out = attend_rows(query4, key_rows, value_rows, allowed, (D // HEADS) ** (-0.5))
    mixed = pieces_out.reshape(tokens, query_heads * HEAD_DIM)
    proj_part = jnp.dot(mixed, w_out, preferred_element_type=jnp.float32)
    attn_sum = lax.psum(proj_part, "heads")
    attn_local = attn_sum.astype(jnp.bfloat16)
    attn_proj, x_full = (
        lax.all_gather(attn_local, "width", axis=1, tiled=True),
        lax.all_gather(x_in, "width", axis=1, tiled=True),
    )
    proj_float = attn_proj.astype(jnp.float32)
    inverse_post = lax.rsqrt(jnp.sum(proj_float * proj_float, axis=1) / D + norm_eps)
    resid = (x_full.astype(jnp.float32) + proj_float * inverse_post[:, None] * post_gain).astype(
        jnp.bfloat16
    )
    centered = (resid.astype(jnp.float32) - dec_bias).astype(jnp.bfloat16)
    pre_acts = jnp.dot(centered, enc_weight, preferred_element_type=jnp.float32) + enc_bias
    latent_acts = jnp.maximum(pre_acts, 0.0).astype(jnp.bfloat16)
    row_norms = jnp.sqrt(jnp.sum(jnp.square(dec_weight.astype(jnp.float32)), axis=1) + norm_eps)
    act_sums = jnp.sum(latent_acts.astype(jnp.float32), axis=0)
    penalty_part = jnp.sum(act_sums * row_norms)
    recon_part = jnp.dot(latent_acts, dec_weight, preferred_element_type=jnp.float32)
    recon = lax.psum(recon_part, ("heads", "width", "sae")) + dec_bias
    error = recon - resid.astype(jnp.float32)
    squares_total = jnp.sum(error * error)
    penalty_total = lax.psum(penalty_part, ("heads", "width", "sae"))
    grad_recon = (2.0 / tokens * error).astype(jnp.bfloat16)
    total_loss = (squares_total + l1_weight * penalty_total) / (tokens * D)
    upstream = lax.dot_general(
        grad_recon, dec_weight, (((1,), (1,)), ((), ())), preferred_element_type=jnp.float32
    )
    grad_pre = jnp.where(pre_acts > 0, upstream + l1_weight * row_norms / tokens, 0.0).astype(
        jnp.bfloat16
    )
    grad_enc = lax.dot_general(
        centered, grad_pre, (((0,), (0,)), ((), ())), preferred_element_type=jnp.float32
    ).astype(jnp.bfloat16)
    decoder_term = lax.dot_general(
        latent_acts, grad_recon, (((0,), (0,)), ((), ())), preferred_element_type=jnp.float32
    )
    grad_dec = (
        decoder_term
        + l1_weight
        / tokens
        * act_sums[:, None]
        * dec_weight.astype(jnp.float32)
        / row_norms[:, None]
    ).astype(jnp.bfloat16)
    return (grad_enc, grad_dec, total_loss)


def solution(mesh):
    placed = (
        P(None, "width"),
        P(),
        P("width"),
        P("width", "heads"),
        P("width", "heads"),
        P("width", "heads"),
        P("heads", "width"),
        P(),
        P(None, ("heads", "width", "sae")),
        P(("heads", "width", "sae")),
        P(("heads", "width", "sae"), None),
        P(),
    )
    return jax.shard_map(
        per_device,
        mesh=mesh,
        in_specs=placed,
        out_specs=(P(None, ("heads", "width", "sae")), P(("heads", "width", "sae"), None), P()),
        check_vma=False,
    )
```

profile of v0, /device:TPU:1, one launch (start us, length us, event | category | flops | bytes accessed | tf_op | source)
XLA Modules:
  0.0 471.6 jit_solution(9375944868353371698)
XLA Ops:
  7.2 0.0 copy-start
  7.2 0.0 copy-start.3
  7.2 0.0 copy-start.11
  7.2 0.0 copy-start.10
  7.2 0.0 copy-start.13
  7.2 0.0 all-reduce.7.cloned.1.call-start
  7.3 3.6 fusion.23
  10.9 2.7 fusion.25
  13.6 0.0 copy-done.3
  13.6 0.0 copy-done.11
  13.6 1.3 fusion.27
  14.9 0.0 all-reduce.7.cloned.1.call-update
  15.0 0.0 all-gather.5.cloned.1.call-start
  15.0 0.2 reduce-window.8
  15.2 0.3 fusion.14
  15.5 9.5 %psum.50 = f32[512]{0:T(512)S(1)} all-reduce(f32[512]{0:T(512)S(1)} %fusion.14), channel_id=1, replica_groups=mesh['heads'=8,'width'=4,'sae'=4] {'width'}, use_global_device_ids=true, to_apply=%region_2.3 | all-reduce | flops 512 | bytes 4096 | tf_op jit(solution)/shard_map/psum | solution.py:73
  25.1 0.1 convert_reduce_fusion.1
  25.2 0.9 fusion.22
  26.1 1.7 multiply_cosine_fusion
  27.8 49.0 %all-reduce.7.cloned.1.call-done = (f32[512,256]{1,0:T(8,128)}, f32[512,512]{1,0:T(8,128)}, f32[512,256]{1,0:T(8,128)}) async-done(((f32[512,256]{1,0:T(8,128)}, f32[512,512]{1,0:T(8,128)}, f32[512,256]{1,0:T(8,128)}), (f32[512,256]{1,0:T(8,128)}, f32[512,512]{1,0:T(8,128)}, f32[512,256]{1,0:T(8,128)})) %all-reduce.7.cloned.1.call-update) | async-done | bytes 2097168 | tf_op jit(solution)/shard_map/psum | solution.py:73
  76.9 2.1 broadcast_multiply_fusion.1
  78.9 0.3 reshape.168
  79.2 1.5 fusion.40
  80.7 1.4 broadcast_multiply_fusion
  82.1 0.4 reshape.169
  82.4 0.0 copy-start.6
  82.4 0.0 copy-start.5
  82.5 1.8 subtract_convert_fusion
  84.3 0.1 copy.23
  84.3 0.1 copy.24
  84.4 0.1 copy.30
  84.6 0.0 copy-done.5
  84.6 1.3 subtract_convert_fusion.1
  85.9 0.0 copy-start.7
  85.9 2.9 fusion.12
  88.8 1.6 fusion.21
  90.4 0.9 fusion.41
  91.3 0.0 copy-start.8
  91.3 52.5 %all-reduce.8 = bf16[512,1152]{1,0:T(8,128)(2,1)} all-reduce(f32[512,1152]{1,0:T(8,128)S(1)} %fusion.41), channel_id=1, replica_groups=mesh['heads'=8,'width'=4,'sae'=4] {'heads'}, use_global_device_ids=true, to_apply=%region_8.9 | all-reduce | flops 589824 | bytes 3538944 | tf_op jit(solution)/shard_map/psum | solution.py:92
  143.8 0.0 all-gather.5.cloned.1.call-update
  143.8 0.0 all-gather.3.cloned.1.call-start
  143.8 0.7 all-gather.3.cloned.1.call-update
  144.5 0.2 all-reduce.5.cloned.1.call-start
  144.8 51.8 %all-gather.5.cloned.1.call-done = bf16[512,4608]{1,0:T(8,128)(2,1)} async-done(((bf16[512,1152]{1,0:T(8,128)(2,1)}), bf16[512,4608]{1,0:T(8,128)(2,1)}) %all-gather.5.cloned.1.call-update) | async-done | bytes 4718608 | tf_op jit(solution)/shard_map/all_gather | solution.py:95
  196.6 3.3 fusion
  199.9 0.0 copy-start.12
  200.0 51.3 %all-gather.3.cloned.1.call-done = bf16[512,4608]{1,0:T(8,128)(2,1)} async-done(((bf16[512,1152]{1,0:T(8,128)(2,1)}), bf16[512,4608]{1,0:T(8,128)(2,1)}) %all-gather.3.cloned.1.call-update) | async-done | bytes 4718608 | tf_op jit(solution)/shard_map/all_gather | solution.py:96
  251.3 0.0 copy-done.8
  251.3 5.9 %fusion.3 = bf16[512,4608]{1,0:T(8,128)(2,1)S(1)} fusion(bf16[512,4608]{1,0:T(8,128)(2,1)} %all-gather.5.cloned.1.call-done, bf16[512,4608]{1,0:T(8,128)(2,1)} %all-gather.3.cloned.1.call-done, f32[4608]{0:T(1024)S(1)} %copy-done.8, f32[512]{0:T(512)S(1)} %add_rsqrt_fusion), kind=kLoop, calls=%fused_computation.9 | loop fusion | flops 14155776 | bytes 14176256 | tf_op jit(solution)/shard_map/convert_element_type | solution.py:100
  257.2 0.0 copy-start.2
  257.2 0.0 slice-start.1
  257.3 6.4 %convert_reduce_fusion = (f32[512]{0:T(512)S(1)}, f32[512,512]{1,0:T(8,128)S(1)}) fusion(f32[512]{0:T(512)S(1)} %copy-done.12, bf16[4608,512]{1,0:T(8,128)(2,1)} %param.20, bf16[512,4608]{1,0:T(8,128)(2,1)S(1)} %fusion.3, f32[4608]{0:T(1024)S(1)} %copy-done.9), kind=kOutput, calls=%fused_computation.32 | convolution fusion | flops 2424045056 | bytes 10508288 | tf_op jit(solution)/shard_map/dot_general | solution.py:104
  263.7 5.1 %fusion.39 = f32[512,4608]{1,0:T(8,128)} fusion(bf16[512,4608]{1,0:T(8,128)(2,1)S(1)} %bitcast.41, f32[512,512]{1,0:T(8,128)S(1)} %get-tuple-element.25), kind=kOutput, calls=%fused_computation.69 | convolution fusion | flops 2416443392 | bytes 15204352 | tf_op jit(solution)/shard_map/dot_general | solution.py:109
  268.8 0.0 all-reduce.5.cloned.1.call-update
  268.8 3.3 fusion.5
  272.2 0.6 multiply_reduce_fusion.1
  272.8 65.8 %psum.55 = f32[]{:T(128)} all-reduce(f32[]{:T(128)} %get-tuple-element.16), channel_id=1, replica_groups=mesh['heads'=8,'width'=4,'sae'=4] {'heads','width','sae'}, use_global_device_ids=true, to_apply=%region_15.16 | all-reduce | flops 1 | bytes 8 | tf_op jit(solution)/shard_map/psum | solution.py:113
  339.2 94.4 %all-reduce.5.cloned.1.call-done = f32[512,4608]{1,0:T(8,128)} async-done(((f32[512,4608]{1,0:T(8,128)}), f32[512,4608]{1,0:T(8,128)}) %all-reduce.5.cloned.1.call-update) | async-done | bytes 9437200 | tf_op jit(solution)/shard_map/psum | solution.py:110
  433.6 8.4 %multiply_reduce_fusion = (f32[]{:T(128)}, bf16[512,4608]{1,0:T(8,128)(2,1)S(1)}) fusion(bf16[512,4608]{1,0:T(8,128)(2,1)} %copy-done.2, f32[512,4608]{1,0:T(8,128)} %all-reduce.5.cloned.1.call-done, f32[4608]{0:T(1024)S(1)} %copy-done.9), kind=kLoop, calls=%fused_computation.15 | loop fusion | flops 16515071 | bytes 18892804 | tf_op jit(solution)/shard_map/reduce_sum | solution.py:112
  442.0 6.7 %fusion.20 = bf16[512,512]{1,0:T(8,128)(2,1)S(1)} fusion(bf16[512,4608]{1,0:T(8,128)(2,1)S(1)} %get-tuple-element.7, bf16[512,4608]{1,0:T(8,128)(2,1)} %param.22, f32[512,512]{1,0:T(8,128)S(1)} %get-tuple-element.25, f32[512]{0:T(512)S(1)} %get-tuple-element.17), kind=kOutput, calls=%fused_computation.30 | convolution fusion | flops 2416967680 | bytes 11012096 | tf_op jit(solution)/shard_map/dot_general | solution.py:116
  448.7 6.8 %convolution_convert_fusion = bf16[4608,512]{1,0:T(8,128)(2,1)} fusion(bf16[512,512]{1,0:T(8,128)(2,1)S(1)} %fusion.20, bf16[512,4608]{1,0:T(8,128)(2,1)} %copy-done.2, f32[4608]{0:T(1024)S(1)} %copy-done.9), kind=kOutput, calls=%fused_computation.17 | convolution fusion | flops 2425356288 | bytes 9979904 | tf_op jit(solution)/shard_map/dot_general | solution.py:122
  456.1 0.0 copy-start.1
  456.1 7.8 %fusion.8 = bf16[512,4608]{1,0:T(8,128)(2,1)} fusion(bf16[512,4608]{1,0:T(8,128)(2,1)} %param.22, bf16[512,4608]{1,0:T(8,128)(2,1)} %copy-done.4, f32[512]{0:T(512)S(1)} %get-tuple-element.18, f32[512]{0:T(512)S(1)} %get-tuple-element.19, f32[512,512]{1,0:T(8,128)S(1)} %get-tuple-element.25), kind=kOutput, calls=%fused_computation.14 | convolution fusion | flops 2428239872 | bytes 15208448 | tf_op jit(solution)/shard_map/dot_general | solution.py:125
  463.9 0.0 copy-done.1
  (19 shorter events, 0.1 us)
Async XLA Ops:
  7.2 83.3 %copy-start = (bf16[512,1152]{1,0:T(8,128)(2,1)S(1)}, bf16[512,1152]{1,0:T(8,128)(2,1)}, u32[]{:S(2)}) copy-start(bf16[512,1152]{1,0:T(8,128)(2,1)} %param.18) | copy-start | bytes 3538948
  7.2 6.5 %copy-start.3 = (bf16[512,1152]{1,0:T(8,128)(2,1)S(1)}, bf16[512,1152]{1,0:T(8,128)(2,1)}, u32[]{:S(2)}) copy-start(bf16[512,1152]{1,0:T(8,128)(2,1)} %param.12) | copy-start | bytes 3538948
  7.2 6.4 %copy-start.11 = (f32[1152]{0:T(1024)S(1)}, f32[1152]{0:T(1024)}, u32[]{:S(2)}) copy-start(f32[1152]{0:T(1024)} %param.14) | copy-start | bytes 13828
  7.2 6.4 %copy-start.10 = (bf16[1152,256]{1,0:T(8,128)(2,1)S(1)}, bf16[1152,256]{1,0:T(8,128)(2,1)}, u32[]{:S(2)}) copy-start(bf16[1152,256]{1,0:T(8,128)(2,1)} %param.17) | copy-start | bytes 1769476
  7.2 7.8 %copy-start.13 = (s32[4]{0:T(128)S(1)}, s32[4]{0:T(128)}, u32[]{:S(2)}) copy-start(s32[4]{0:T(128)} %param.13) | copy-start | bytes 52
  7.2 69.6 %all-reduce.7.cloned.1.call-start = ((), (), s32[]{:S(2)}) async-start(), calls=%async_computation.3 | async-start | bytes 4194304 | tf_op jit(solution)/shard_map/psum | solution.py:73
  15.0 181.6 %all-gather.5.cloned.1.call-start = ((), (), s32[]{:S(2)}) async-start(), calls=%async_computation.1 | async-start | bytes 5898240 | tf_op jit(solution)/shard_map/all_gather | solution.py:95
  82.4 2.0 copy-start.6
  82.4 2.1 copy-start.5
  85.9 2.9 copy-start.7
  91.3 160.0 %copy-start.8 = (f32[4608]{0:T(1024)S(1)}, f32[4608]{0:T(1024)}, u32[]{:S(2)}) copy-start(f32[4608]{0:T(1024)} %param.19) | copy-start | bytes 55300
  143.8 107.5 %all-gather.3.cloned.1.call-start = ((), (), s32[]{:S(2)}) async-start(), calls=%async_computation | async-start | bytes 5898240 | tf_op jit(solution)/shard_map/all_gather | solution.py:96
  144.5 289.1 %all-reduce.5.cloned.1.call-start = ((), (), s32[]{:S(2)}) async-start(), calls=%async_computation.2 | async-start | bytes 18874368 | tf_op jit(solution)/shard_map/psum | solution.py:110
  199.9 57.3 %copy-start.9 = (f32[4608]{0:T(1024)S(1)}, f32[4608]{0:T(1024)}, u32[]{:S(2)}) copy-start(f32[4608]{0:T(1024)} %param.23) | copy-start | bytes 55300
  199.9 57.3 %copy-start.12 = (f32[512]{0:T(512)S(1)}, f32[512]{0:T(512)}, u32[]{:S(2)}) copy-start(f32[512]{0:T(512)} %param.21) | copy-start | bytes 6148
  251.3 12.4 %slice-start = ((s8[4718592]{0:T(1024)(128)(4,1)}), s8[4194304]{0:T(1024)(128)(4,1)S(1)}, s32[]{:S(2)}) async-start(s8[4718592]{0:T(1024)(128)(4,1)} %bitcast.40), calls=%async_computation.4 | async-start | bytes 8388608
  257.2 6.4 %copy-start.2 = (bf16[512,4608]{1,0:T(8,128)(2,1)}, bf16[512,4608]{1,0:T(8,128)(2,1)S(1)}, u32[]{:S(2)}) copy-start(bf16[512,4608]{1,0:T(8,128)(2,1)S(1)} %fusion.3) | copy-start | bytes 14155780
  257.2 6.5 %slice-start.1 = ((s8[4718592]{0:T(1024)(128)(4,1)}), s8[524288]{0:T(1024)(128)(4,1)S(1)}, s32[]{:S(2)}) async-start(s8[4718592]{0:T(1024)(128)(4,1)} %bitcast.40), calls=%async_computation.5 | async-start | bytes 1048576
  442.0 6.7 %copy-start.4 = (bf16[512,4608]{1,0:T(8,128)(2,1)}, bf16[512,4608]{1,0:T(8,128)(2,1)S(1)}, u32[]{:S(2)}) copy-start(bf16[512,4608]{1,0:T(8,128)(2,1)S(1)} %get-tuple-element.7) | copy-start | bytes 14155780
  456.1 7.9 %copy-start.1 = (bf16[512,1152]{1,0:T(8,128)(2,1)S(1)}, bf16[512,1152]{1,0:T(8,128)(2,1)}, u32[]{:S(2)}) copy-start(bf16[512,1152]{1,0:T(8,128)(2,1)} %param.18) | copy-start | bytes 3538948
Sparse Core Ops, SparseCore 0:
  15.1 61.7 all-reduce.6
  143.9 52.6 all-gather.4
  198.3 52.9 all-gather.2
  268.9 164.6 all-reduce.4
where the time goes:
time: 472 us
  waiting for transfers between devices  247 us (52%)
  blocking collectives  128 us (27%)
  matrix products  45.7 us (10%)
  other arithmetic  31.4 us (7%)
  between operations  16.5 us (3%)
    psum x1, waiting for transfers between devices, per_device(): recon = lax.psum(recon_part, ('heads', 'width', 'sae')) + dec_bias  94.4 us
    psum x1, blocking collectives, per_device(): penalty_total = lax.psum(penalty_part, ('heads', 'width', 'sae'))  65.8 us
    psum x1, blocking collectives, per_device(): attn_sum = lax.psum(proj_part, 'heads')  52.5 us
    all_gather x1, waiting for transfers between devices, per_device(): lax.all_gather(attn_local, 'width', axis=1, tiled=True)  51.8 us
    all_gather x1, waiting for transfers between devices, per_device(): lax.all_gather(x_in, 'width', axis=1, tiled=True)  51.3 us
    psum x1, waiting for transfers between devices, per_device(): lax.psum((query_part, key_part, value_part, square_part), 'width')  49 us
    psum x1, blocking collectives, per_device(): lax.psum((query_part, key_part, value_part, square_part), 'width')  9.54 us
  transfers between devices with their start and end apart: 4, of which 4 were waited for; matrix products, arithmetic and copies ran while one was open for 2% of the time, Pallas kernels for 0%

commit v1 on v0

--- a/solution.py
+++ b/solution.py
@@ -2,6 +2,7 @@
 import jax.numpy as jnp
 from jax import lax
 from jax.sharding import PartitionSpec as P
+from jax.lax import all_gather
 
 D = 4608
 HEADS = 32
@@ -10,6 +11,11 @@
 soft_cap = 50.0
 rope_base = 10000.0
 l1_weight = 3.0
+
+
+def prepare_slabs(shard_in):
+    local_next = jnp.concatenate(all_gather(shard_in, axis_name="width"), 1)
+    return local_next
 
 
 def rotary(values, position):
@@ -93,7 +99,7 @@
     attn_local = attn_sum.astype(jnp.bfloat16)
     attn_proj, x_full = (
         lax.all_gather(attn_local, "width", axis=1, tiled=True),
-        lax.all_gather(x_in, "width", axis=1, tiled=True),
+        prepare_slabs(x_in),
     )
     proj_float = attn_proj.astype(jnp.float32)
     inverse_post = lax.rsqrt(jnp.sum(proj_float * proj_float, axis=1) / D + norm_eps)

time: 472 us -> 423 us (0.90)
  waiting for transfers between devices: 247 us -> 178 us
  local copies, waits for them, and re-layouts: 2.52 us -> 22 us
    all_gather x1, waiting for transfers between devices: 51.3 us -> 0.02 us  [prepare_slabs(): local_next = jnp.concatenate(all_gather(shard_in, axis_name='width'), 1)]
    all_gather x1, waiting for transfers between devices: 51.8 us -> 33.6 us  [per_device(): lax.all_gather(attn_local, 'width', axis=1, tiled=True)]
    convert_element_type x0 -> x1, local copies, waits for them, and re-layouts: none -> 9.77 us  [per_device(): x_full.astype(jnp.float32) + proj_float * inverse_post[:, None] * post_gain]
    unnamed x32 -> x33, local copies, waits for them, and re-layouts: 0.09 us -> 8.82 us
  transfers between devices with their start and end apart: 4 -> 4, of which waited for: 4 -> 3; matrix products, arithmetic and copies ran while one was open for 2% -> 9% of each run, Pallas kernels for 0% -> 0%
where the time goes in v1:
time: 423 us; the launch traced here: 422 us
  waiting for transfers between devices  178 us (42%)
  blocking collectives  130 us (31%)
  matrix products  45.4 us (11%)
  other arithmetic  30.7 us (7%)
  local copies, waits for them, and re-layouts  22 us (5%)
  between operations  16.4 us (4%)
    psum x1, waiting for transfers between devices, per_device(): recon = lax.psum(recon_part, ('heads', 'width', 'sae')) + dec_bias  94.3 us
    psum x1, blocking collectives, per_device(): penalty_total = lax.psum(penalty_part, ('heads', 'width', 'sae'))  65.8 us
    psum x1, blocking collectives, per_device(): attn_sum = lax.psum(proj_part, 'heads')  54.5 us
    psum x1, waiting for transfers between devices, per_device(): lax.psum((query_part, key_part, value_part, square_part), 'width')  49 us
    all_gather x1, waiting for transfers between devices, per_device(): lax.all_gather(attn_local, 'width', axis=1, tiled=True)  33.6 us
    convert_element_type x1, local copies, waits for them, and re-layouts, per_device(): x_full.astype(jnp.float32) + proj_float * inverse_post[:, None] * post_gain  9.77 us
    psum x1, blocking collectives, per_device(): lax.psum((query_part, key_part, value_part, square_part), 'width')  9.55 us
    unnamed x33, local copies, waits for them, and re-layouts  8.82 us
  transfers between devices with their start and end apart: 4, of which 3 were waited for; matrix products, arithmetic and copies ran while one was open for 9% of the time, Pallas kernels for 0%

profile of v1, /device:TPU:1, one launch (start us, length us, event | category | flops | bytes accessed | tf_op | source)
XLA Modules:
  0.0 422.4 jit_solution(1412428543357622694)
XLA Ops:
  7.2 0.0 copy-start
  7.2 0.0 copy-start.3
  7.2 0.0 copy-start.11
  7.2 0.0 all-reduce.7.cloned.1.call-start
  7.3 0.0 copy-start.10
  7.3 3.6 fusion.23
  10.9 2.8 fusion.25
  13.7 0.0 copy-done.3
  13.7 0.0 copy-done.11
  13.7 0.0 copy-done.10
  13.7 1.3 fusion.27
  15.0 0.0 all-reduce.7.cloned.1.call-update
  15.1 0.0 all-gather.6.cloned.1.call-start
  15.1 0.7 all-gather.6.cloned.1.call-update
  15.8 0.0 all-gather.4.cloned.1.call-start
  15.9 0.0 copy-done.13
  15.9 0.2 reduce-window.8
  16.0 0.3 fusion.14
  16.4 9.5 %psum.50 = f32[512]{0:T(512)S(1)} all-reduce(f32[512]{0:T(512)S(1)} %fusion.14), channel_id=1, replica_groups=mesh['heads'=8,'width'=4,'sae'=4] {'width'}, use_global_device_ids=true, to_apply=%region_2.3 | all-reduce | flops 512 | bytes 4096 | tf_op jit(solution)/shard_map/psum | solution.py:79
  25.9 0.1 convert_reduce_fusion.1
  26.0 0.9 fusion.22
  26.9 1.0 multiply_cosine_fusion
  27.9 49.0 %all-reduce.7.cloned.1.call-done = (f32[512,256]{1,0:T(8,128)}, f32[512,512]{1,0:T(8,128)}, f32[512,256]{1,0:T(8,128)}) async-done(((f32[512,256]{1,0:T(8,128)}, f32[512,512]{1,0:T(8,128)}, f32[512,256]{1,0:T(8,128)}), (f32[512,256]{1,0:T(8,128)}, f32[512,512]{1,0:T(8,128)}, f32[512,256]{1,0:T(8,128)})) %all-reduce.7.cloned.1.call-update) | async-done | bytes 2097168 | tf_op jit(solution)/shard_map/psum | solution.py:79
  76.9 1.3 broadcast_multiply_fusion.1
  78.3 0.3 reshape.172
  78.6 2.3 broadcast_multiply_fusion
  80.9 1.6 reshape.173
  82.5 0.8 subtract_convert_fusion
  83.3 0.1 copy.26
  83.3 0.1 copy.25
  83.4 0.8 copy.32
  84.3 0.6 fusion.40
  84.9 0.1 subtract_convert_fusion.1
  85.0 0.0 copy-start.7
  85.0 2.9 fusion.12
  87.9 0.0 copy-done.6
  87.9 0.0 copy-done.7
  87.9 1.6 fusion.21
  89.5 0.9 fusion.41
  90.4 54.5 %all-reduce.8 = bf16[512,1152]{1,0:T(8,128)(2,1)} all-reduce(f32[512,1152]{1,0:T(8,128)S(1)} %fusion.41), channel_id=1, replica_groups=mesh['heads'=8,'width'=4,'sae'=4] {'heads'}, use_global_device_ids=true, to_apply=%region_8.9 | all-reduce | flops 589824 | bytes 3538944 | tf_op jit(solution)/shard_map/psum | solution.py:98
  144.8 0.0 all-gather.4.cloned.1.call-update
  144.9 0.2 all-reduce.5.cloned.1.call-start
  145.1 0.0 all-gather.6.cloned.1.call-done
  145.1 9.8 %copy.22 = f32[4,512,1152]{2,0,1:T(4,128)} copy(bf16[4,512,1152]{2,1,0:T(8,128)(2,1)} %bitcast.49) | data formatting | bytes 14155776 | tf_op jit(solution)/shard_map/convert_element_type | solution.py:106
  154.9 8.5 %copy.35 = f32[64,8,4,1152]{3,1,2,0:T(8,128)} copy(f32[64,8,4,1152]{3,2,1,0:T(4,128)} %bitcast.46) | data formatting | bytes 18874368
  163.4 33.6 %all-gather.4.cloned.1.call-done = bf16[512,4608]{1,0:T(8,128)(2,1)} async-done(((bf16[512,1152]{1,0:T(8,128)(2,1)}), bf16[512,4608]{1,0:T(8,128)(2,1)}) %all-gather.4.cloned.1.call-update) | async-done | bytes 4718608 | tf_op jit(solution)/shard_map/all_gather | solution.py:101
  197.0 3.5 fusion
  200.5 0.3 copy-done.2
  200.7 7.8 %fusion.3 = bf16[512,4608]{1,0:T(8,128)(2,1)} fusion(f32[512,4608]{1,0:T(8,128)} %bitcast.45, bf16[512,4608]{1,0:T(8,128)(2,1)S(1)} %copy-done.2, f32[4608]{0:T(1024)S(1)} %copy-done.8, f32[512]{0:T(512)S(1)} %add_rsqrt_fusion), kind=kLoop, calls=%fused_computation.9 | loop fusion | flops 11796480 | bytes 18894848 | tf_op jit(solution)/shard_map/convert_element_type | solution.py:106
  208.6 0.0 copy-done.9
  208.6 6.0 %convert_reduce_fusion = (f32[512]{0:T(512)S(1)}, f32[512,512]{1,0:T(8,128)S(1)}) fusion(f32[512]{0:T(512)S(1)} %copy-done.12, bf16[4608,512]{1,0:T(8,128)(2,1)} %param.20, bf16[512,4608]{1,0:T(8,128)(2,1)} %fusion.3, f32[4608]{0:T(1024)S(1)} %copy-done.9), kind=kOutput, calls=%fused_computation.32 | convolution fusion | flops 2424045056 | bytes 10508288 | tf_op jit(solution)/shard_map/dot_general | solution.py:110
  214.6 0.0 slice-done
  214.6 0.0 slice-done.1
  214.6 5.1 %fusion.39 = f32[512,4608]{1,0:T(8,128)} fusion(bf16[512,4608]{1,0:T(8,128)(2,1)S(1)} %bitcast.48, f32[512,512]{1,0:T(8,128)S(1)} %get-tuple-element.25), kind=kOutput, calls=%fused_computation.69 | convolution fusion | flops 2416443392 | bytes 15204352 | tf_op jit(solution)/shard_map/dot_general | solution.py:115
  219.7 0.0 all-reduce.5.cloned.1.call-update
  219.7 3.3 fusion.5
  223.1 0.6 multiply_reduce_fusion.1
  223.7 65.8 %psum.55 = f32[]{:T(128)} all-reduce(f32[]{:T(128)} %get-tuple-element.16), channel_id=1, replica_groups=mesh['heads'=8,'width'=4,'sae'=4] {'heads','width','sae'}, use_global_device_ids=true, to_apply=%region_15.16 | all-reduce | flops 1 | bytes 8 | tf_op jit(solution)/shard_map/psum | solution.py:119
  290.1 94.3 %all-reduce.5.cloned.1.call-done = f32[512,4608]{1,0:T(8,128)} async-done(((f32[512,4608]{1,0:T(8,128)}), f32[512,4608]{1,0:T(8,128)}) %all-reduce.5.cloned.1.call-update) | async-done | bytes 9437200 | tf_op jit(solution)/shard_map/psum | solution.py:116
  384.4 8.4 %multiply_reduce_fusion = (f32[]{:T(128)}, bf16[512,4608]{1,0:T(8,128)(2,1)S(1)}) fusion(bf16[512,4608]{1,0:T(8,128)(2,1)} %fusion.3, f32[512,4608]{1,0:T(8,128)} %all-reduce.5.cloned.1.call-done, f32[4608]{0:T(1024)S(1)} %copy-done.9), kind=kLoop, calls=%fused_computation.15 | loop fusion | flops 16515071 | bytes 18892804 | tf_op jit(solution)/shard_map/reduce_sum | solution.py:118
  392.8 6.7 %fusion.20 = bf16[512,512]{1,0:T(8,128)(2,1)S(1)} fusion(bf16[512,4608]{1,0:T(8,128)(2,1)S(1)} %get-tuple-element.7, bf16[512,4608]{1,0:T(8,128)(2,1)} %param.22, f32[512,512]{1,0:T(8,128)S(1)} %get-tuple-element.25, f32[512]{0:T(512)S(1)} %get-tuple-element.17), kind=kOutput, calls=%fused_computation.30 | convolution fusion | flops 2416967680 | bytes 11012096 | tf_op jit(solution)/shard_map/dot_general | solution.py:122
  399.5 6.7 %convolution_convert_fusion = bf16[4608,512]{1,0:T(8,128)(2,1)} fusion(bf16[512,512]{1,0:T(8,128)(2,1)S(1)} %fusion.20, bf16[512,4608]{1,0:T(8,128)(2,1)} %fusion.3, f32[4608]{0:T(1024)S(1)} %copy-done.9), kind=kOutput, calls=%fused_computation.17 | convolution fusion | flops 2425356288 | bytes 9979904 | tf_op jit(solution)/shard_map/dot_general | solution.py:128
  406.9 0.0 copy-start.1
  406.9 7.8 %fusion.8 = bf16[512,4608]{1,0:T(8,128)(2,1)} fusion(bf16[512,4608]{1,0:T(8,128)(2,1)} %param.22, bf16[512,4608]{1,0:T(8,128)(2,1)} %copy-done.5, f32[512]{0:T(512)S(1)} %get-tuple-element.18, f32[512]{0:T(512)S(1)} %get-tuple-element.19, f32[512,512]{1,0:T(8,128)S(1)} %get-tuple-element.25), kind=kOutput, calls=%fused_computation.14 | convolution fusion | flops 2428239872 | bytes 15208448 | tf_op jit(solution)/shard_map/dot_general | solution.py:131
  (21 shorter events, 0.1 us)
Async XLA Ops:
  7.2 82.3 %copy-start = (bf16[512,1152]{1,0:T(8,128)(2,1)S(1)}, bf16[512,1152]{1,0:T(8,128)(2,1)}, u32[]{:S(2)}) copy-start(bf16[512,1152]{1,0:T(8,128)(2,1)} %param.18) | copy-start | bytes 3538948
  7.2 6.5 %copy-start.3 = (bf16[512,1152]{1,0:T(8,128)(2,1)S(1)}, bf16[512,1152]{1,0:T(8,128)(2,1)}, u32[]{:S(2)}) copy-start(bf16[512,1152]{1,0:T(8,128)(2,1)} %param.12) | copy-start | bytes 3538948
  7.2 6.5 %copy-start.11 = (f32[1152]{0:T(1024)S(1)}, f32[1152]{0:T(1024)}, u32[]{:S(2)}) copy-start(f32[1152]{0:T(1024)} %param.14) | copy-start | bytes 13828
  7.2 69.7 %all-reduce.7.cloned.1.call-start = ((), (), s32[]{:S(2)}) async-start(), calls=%async_computation.3 | async-start | bytes 4194304 | tf_op jit(solution)/shard_map/psum | solution.py:79
  7.3 6.5 %copy-start.10 = (bf16[1152,256]{1,0:T(8,128)(2,1)S(1)}, bf16[1152,256]{1,0:T(8,128)(2,1)}, u32[]{:S(2)}) copy-start(bf16[1152,256]{1,0:T(8,128)(2,1)} %param.17) | copy-start | bytes 1769476
  10.9 5.0 %copy-start.13 = (s32[4]{0:T(128)S(1)}, s32[4]{0:T(128)}, u32[]{:S(2)}) copy-start(s32[4]{0:T(128)} %param.13) | copy-start | bytes 52
  10.9 5.2 %copy-start.4 = (bf16[512,1152]{1,0:T(8,128)(2,1)S(1)}, bf16[512,1152]{1,0:T(8,128)(2,1)}, u32[]{:S(2)}) copy-start(bf16[512,1152]{1,0:T(8,128)(2,1)} %param.12) | copy-start | bytes 3538948
  15.1 130.1 %all-gather.6.cloned.1.call-start = ((), (), s32[]{:S(2)}) async-start(), calls=%async_computation.2 | async-start | bytes 5898240 | tf_op jit(solution)/shard_map/all_gather | solution.py:17
  15.8 181.2 %all-gather.4.cloned.1.call-start = ((), (), s32[]{:S(2)}) async-start(), calls=%async_computation | async-start | bytes 5898240 | tf_op jit(solution)/shard_map/all_gather | solution.py:101
  85.0 2.9 copy-start.6
  85.0 2.9 copy-start.7
  144.9 239.6 %all-reduce.5.cloned.1.call-start = ((), (), s32[]{:S(2)}) async-start(), calls=%async_computation.1 | async-start | bytes 18874368 | tf_op jit(solution)/shard_map/psum | solution.py:116
  154.9 45.6 %copy-start.8 = (f32[4608]{0:T(1024)S(1)}, f32[4608]{0:T(1024)}, u32[]{:S(2)}) copy-start(f32[4608]{0:T(1024)} %param.19) | copy-start | bytes 55300
  197.0 3.8 copy-start.2
  200.7 7.8 %copy-start.9 = (f32[4608]{0:T(1024)S(1)}, f32[4608]{0:T(1024)}, u32[]{:S(2)}) copy-start(f32[4608]{0:T(1024)} %param.23) | copy-start | bytes 55300
  200.7 7.8 %copy-start.12 = (f32[512]{0:T(512)S(1)}, f32[512]{0:T(512)}, u32[]{:S(2)}) copy-start(f32[512]{0:T(512)} %param.21) | copy-start | bytes 6148
  200.7 13.9 %slice-start = ((s8[4718592]{0:T(1024)(128)(4,1)}), s8[524288]{0:T(1024)(128)(4,1)S(1)}, s32[]{:S(2)}) async-start(s8[4718592]{0:T(1024)(128)(4,1)} %bitcast.47), calls=%async_computation.4 | async-start | bytes 1048576
  208.6 6.1 %slice-start.1 = ((s8[4718592]{0:T(1024)(128)(4,1)}), s8[4194304]{0:T(1024)(128)(4,1)S(1)}, s32[]{:S(2)}) async-start(s8[4718592]{0:T(1024)(128)(4,1)} %bitcast.47), calls=%async_computation.5 | async-start | bytes 8388608
  392.8 6.7 %copy-start.5 = (bf16[512,4608]{1,0:T(8,128)(2,1)}, bf16[512,4608]{1,0:T(8,128)(2,1)S(1)}, u32[]{:S(2)}) copy-start(bf16[512,4608]{1,0:T(8,128)(2,1)S(1)} %get-tuple-element.7) | copy-start | bytes 14155780
  406.9 7.9 %copy-start.1 = (bf16[512,1152]{1,0:T(8,128)(2,1)S(1)}, bf16[512,1152]{1,0:T(8,128)(2,1)}, u32[]{:S(2)}) copy-start(bf16[512,1152]{1,0:T(8,128)(2,1)} %param.18) | copy-start | bytes 3538948
Sparse Core Ops, SparseCore 0:
  15.2 61.7 all-reduce.6
  78.6 52.3 all-gather.5
  145.0 51.9 all-gather.3
  219.8 164.5 all-reduce.4
